TPU v7x, 32 devices: a whole 2x2x4 slice. The times are simulated.
32 devices in a mesh: wide: 8 (over z, core), narrow: 4 (over y, x).
Axes of the slice: x: 2, y: 2, z: 4, core: 2. Of those that a mesh axis runs over, the one named last changes fastest.
Arguments:
- tokens: bfloat16 [8192, 2048], P('wide'), may hold values from -4 to 4
- cotangent: bfloat16 [8192, 2048], P('wide'), may hold values from -4 to 4
- noise_emb: float32 [128, 2048], P('wide'), may hold values from -2.5 to 2.5
- offsets: int32 [8, 16], P('wide'), may hold values from 0 to 1024, as said below
- lengths: int32 [8, 16], P('wide'), may hold values from 0 to 1024, as said below
- group_ids: int32 [8, 16], P('wide'), may hold values from 0 to 2, as said below
- group_table: float32 [3, 2048], replicated, may hold values from -2.5 to 2.5
- w_qkv: bfloat16 [3, 2048, 2048], P(None, None, 'narrow'), may hold values from -0.125 to 0.125
- w_out: bfloat16 [2048, 2048], P('narrow'), may hold values from -0.5 to 0.5
- w_up: bfloat16 [2048, 8192], P(None, 'narrow'), may hold values from -0.125 to 0.125
- b_up: float32 [8192], P('narrow'), may hold values from -2.5 to 2.5
- w_down: bfloat16 [8192, 2048], P('narrow'), may hold values from -0.09375 to 0.09375
- w_mod: bfloat16 [2048, 6, 2048], P(None, None, 'narrow'), may hold values from -0.0625 to 0.0625
- b_mod: float32 [6, 2048], P(None, 'narrow'), may hold values from -1.5 to 1.5
Outputs:
- result: bfloat16 [8192, 2048], P('wide')
- grad_tokens: bfloat16 [8192, 2048], P('wide')
- grad_noise: float32 [128, 2048], P('wide')
- grad_group_table: float32 [3, 2048], P(None, 'wide')
- grad_w_qkv: float32 [3, 2048, 2048], P(None, 'wide', 'narrow')
- grad_w_out: float32 [2048, 2048], P('narrow', 'wide')
- grad_w_up: float32 [2048, 8192], P('wide', 'narrow')
- grad_b_up: float32 [8192], P(('narrow', 'wide'))
- grad_w_down: float32 [8192, 2048], P('narrow', 'wide')
- grad_w_mod: float32 [2048, 6, 2048], P('wide', None, 'narrow')
- grad_b_mod: float32 [6, 2048], P(None, ('narrow', 'wide'))
Inputs may be any that keep to these rules, and one draw needn't show every extreme that they name: `offsets`: each index of wide holds images of one length, 1024, 256 or 64 tokens, laid end to end from token 0 and filling its 1024 tokens: slot s starts at s times that length. Slots past the last image start at 1024. Every length occurs on some index of wide. `lengths`: the length of each image slot; 0 for slots past the last image of an index of wide. `group_ids`: 0 on indices of wide with images of 1024 tokens, 1 with 256, 2 with 64, for all slots of that index; every group occurs.
All inputs are finite; a program needn't handle non-finite values.
Results may differ from a plain program's by a relative error of at most 0.018.
Values may be sent and summed in bfloat16 or wider, within the bound.
No kernel may reach another device: no remote copies, remote signals or barrier semaphores. Data moves between devices by JAX's collectives and lax.ppermute only.
A program may use at most 320 MiB of HBM per device.

v0:
```python
import jax
import jax.numpy as jnp
from jax import lax
from jax.sharding import PartitionSpec as P

HEAD_DIM = 128
highest = lax.Precision.HIGHEST


def normalize(values):
    centred = values - jnp.mean(values, axis=-1, keepdims=True)
    recip = lax.rsqrt(jnp.mean(centred * centred, axis=-1, keepdims=True) + 1e-06)
    return (centred * recip, recip)


def norm_back(grad, normed, recip):
    first = jnp.mean(grad, axis=-1, keepdims=True)
    second = jnp.mean(grad * normed, axis=-1, keepdims=True)
    return recip * (grad - first - normed * second)


def gelu_slope(values):
    cumul = 0.5 * (1.0 + lax.erf(values * 0.7071067811865476))
    density = jnp.exp(-0.5 * values * values) * 0.3989422804014327
    return cumul + values * density


def body(
    tokens,
    cotangent,
    noise_emb,
    offsets,
    lengths,
    group_ids,
    group_table,
    w_qkv,
    w_out,
    w_up,
    b_up,
    w_down,
    w_mod,
    b_mod,
):
    f32 = jnp.float32
    half = jnp.bfloat16
    tok_dev, width = tokens.shape
    slots = offsets.shape[1]
    local_width = w_qkv.shape[2]
    heads_here = local_width // HEAD_DIM
    groups = group_table.shape[0]
    positions = jnp.arange(tok_dev, dtype=jnp.int32)[:, None]
    member = ((positions >= offsets) & (positions < offsets + lengths)).astype(f32)
    image_of = jnp.dot(member, jnp.arange(slots, dtype=f32), precision=highest)
    group_hot = (group_ids[0][:, None] == jnp.arange(groups, dtype=jnp.int32)[None, :]).astype(f32)
    cond = noise_emb + jnp.dot(group_hot, group_table, precision=highest)
    silu_low = jax.nn.silu(cond).astype(half)
    mod_local = jnp.dot(
        silu_low, w_mod.reshape(width, 6 * local_width), preferred_element_type=f32
    ) + b_mod.reshape(6 * local_width)
    mod_full = lax.all_gather(
        mod_local.reshape(slots, 6, local_width), "narrow", axis=2, tiled=True
    )

    def per_token(column):
        return jnp.dot(member, mod_full[:, column], precision=highest)

    shift_a = per_token(0)
    scale_a = per_token(1)
    gate_a = per_token(2)
    shift_b = per_token(3)
    scale_b = per_token(4)
    gate_b = per_token(5)
    tok_f = tokens.astype(f32)
    normed_a, recip_a = normalize(tok_f)
    mixed_a = (normed_a * (1.0 + scale_a) + shift_a).astype(half)
    factor = HEAD_DIM ** (-0.5)
    query = (jnp.dot(mixed_a, w_qkv[0], preferred_element_type=f32) * factor).astype(half)
    keys = jnp.dot(mixed_a, w_qkv[1], preferred_element_type=f32).astype(half)
    values = jnp.dot(mixed_a, w_qkv[2], preferred_element_type=f32).astype(half)
    block_rows = min(512, tok_dev)
    blocks = tok_dev // block_rows
    q_blocks = query.reshape(blocks, block_rows, heads_here, HEAD_DIM)
    key_heads = keys.reshape(tok_dev, heads_here, HEAD_DIM)
    value_heads = values.reshape(tok_dev, heads_here, HEAD_DIM)
    image_blocks = image_of.reshape(blocks, block_rows)

    def block_scores(q_block, image_block):
        scores = jnp.einsum("qhd,khd->hqk", q_block, key_heads, preferred_element_type=f32)
        same = image_block[:, None] == image_of[None, :]
        return jnp.where(same[None], scores, -1e30)

    def forward_block(item):
        scores = block_scores(item[0], item[1])
        top = jnp.max(scores, axis=-1, keepdims=True)
        expo = jnp.exp(scores - top)
        total = jnp.sum(expo, axis=-1, keepdims=True)
        probs = expo / total
        out = jnp.einsum(
            "hqk,khd->qhd", probs.astype(half), value_heads, preferred_element_type=f32
        )
        return (out.astype(half), (top + jnp.log(total))[..., 0])

    outs, log_totals = lax.map(forward_block, (q_blocks, image_blocks))
    heads_out = outs.reshape(tok_dev, local_width)
    attended = lax.psum(jnp.dot(heads_out, w_out, preferred_element_type=f32), "narrow")
    middle = tok_f + gate_a * attended
    normed_b, recip_b = normalize(middle)
    mixed_b = (normed_b * (1.0 + scale_b) + shift_b).astype(half)
    hidden_pre = jnp.dot(mixed_b, w_up, preferred_element_type=f32) + b_up
    hidden = jax.nn.gelu(hidden_pre, approximate=False).astype(half)
    mlp_out = lax.psum(
        jnp.dot(hidden, w_down, preferred_element_type=f32).astype(jnp.bfloat16), "narrow"
    ).astype(jnp.float32)
    result = (middle + gate_b * mlp_out).astype(half)
    grad_out = cotangent.astype(f32)
    d_mlp = (grad_out * gate_b).astype(half)
    d_hidden = jnp.dot(d_mlp, w_down.T, preferred_element_type=f32).astype(half)
    d_pre = (d_hidden.astype(f32) * gelu_slope(hidden_pre)).astype(half)
    grad_b_up = jnp.sum(d_pre.astype(f32), axis=0)
    grad_w_down = jnp.dot(hidden.T, d_mlp, preferred_element_type=f32)
    grad_w_up = jnp.dot(mixed_b.T, d_pre, preferred_element_type=f32)
    d_mixed_b = lax.psum(jnp.dot(d_pre, w_up.T, preferred_element_type=f32), "narrow")
    d_middle = grad_out + norm_back(d_mixed_b * (1.0 + scale_b), normed_b, recip_b)
    d_attn = (d_middle * gate_a).astype(half)
    grad_w_out = jnp.dot(heads_out.T, d_attn, preferred_element_type=f32)
    d_heads = jnp.dot(d_attn, w_out.T, preferred_element_type=f32).astype(half)
    d_blocks = d_heads.reshape(blocks, block_rows, heads_here, HEAD_DIM)

    def backward_block(carry, item):
        grad_key, grad_value = carry
        q_block, image_block, d_block, lse_block = item
        probs = jnp.exp(block_scores(q_block, image_block) - lse_block[..., None])
        d_probs = jnp.einsum("qhd,khd->hqk", d_block, value_heads, preferred_element_type=f32)
        inner = jnp.sum(probs * d_probs, axis=-1, keepdims=True)
        d_scores = (probs * (d_probs - inner)).astype(half)
        grad_query = jnp.einsum("hqk,khd->qhd", d_scores, key_heads, preferred_element_type=f32)
        grad_key = grad_key + jnp.einsum(
            "hqk,qhd->khd", d_scores, q_block, preferred_element_type=f32
        )
        grad_value = grad_value + jnp.einsum(
            "hqk,qhd->khd", probs.astype(half), d_block, preferred_element_type=f32
        )
        return ((grad_key, grad_value), grad_query)

    zeros = jnp.zeros((tok_dev, heads_here, HEAD_DIM), f32)
    (grad_key, grad_value), grad_query = lax.scan(
        backward_block, (zeros, zeros), (q_blocks, image_blocks, d_blocks, log_totals)
    )
    d_query = (grad_query.reshape(tok_dev, local_width) * factor).astype(half)
    d_key = grad_key.reshape(tok_dev, local_width).astype(half)
    d_value = grad_value.reshape(tok_dev, local_width).astype(half)
    d_proj = jnp.stack([d_query, d_key, d_value], axis=1)
    grad_w_qkv = jnp.einsum("td,tiv->idv", mixed_a, d_proj, preferred_element_type=f32)
    d_mixed_a = lax.psum(
        jnp.einsum("tiv,idv->td", d_proj, w_qkv, preferred_element_type=f32).astype(jnp.bfloat16),
        "narrow",
    ).astype(jnp.float32)
    grad_tokens = (d_middle + norm_back(d_mixed_a * (1.0 + scale_a), normed_a, recip_a)).astype(
        half
    )
    start = lax.axis_index("narrow") * local_width

    def own(values_in):
        return lax.dynamic_slice_in_dim(values_in, start, local_width, 1)

    token_terms = jnp.stack(
        [
            own(d_mixed_a),
            own(d_mixed_a * normed_a),
            own(d_middle * attended),
            own(d_mixed_b),
            own(d_mixed_b * normed_b),
            own(grad_out * mlp_out),
        ],
        axis=1,
    )
    d_modes = jnp.einsum("ts,tcv->scv", member, token_terms, precision=highest).astype(half)
    flat_modes = d_modes.reshape(slots, 6 * local_width)
    d_silu = lax.psum(
        jnp.dot(
            flat_modes, w_mod.reshape(width, 6 * local_width).T, preferred_element_type=f32
        ).astype(jnp.bfloat16),
        "narrow",
    ).astype(jnp.float32)
    sigma = jax.nn.sigmoid(cond)
    grad_noise = d_silu * sigma * (1.0 + cond * (1.0 - sigma))
    grad_table = jnp.dot(group_hot.T, grad_noise, precision=highest)
    grad_b_mod = jnp.sum(d_modes.astype(f32), axis=0)
    grad_w_mod = jnp.dot(silu_low.T, flat_modes, preferred_element_type=f32).reshape(
        width, 6, local_width
    )
    summed = (
        lax.psum_scatter(
            grad_w_qkv.astype(jnp.bfloat16), "wide", scatter_dimension=1, tiled=True
        ).astype(jnp.float32),
        lax.psum_scatter(
            grad_w_out.astype(jnp.bfloat16), "wide", scatter_dimension=1, tiled=True
        ).astype(jnp.float32),
        lax.psum_scatter(
            grad_w_up.astype(jnp.bfloat16), "wide", scatter_dimension=0, tiled=True
        ).astype(jnp.float32),
        lax.psum_scatter(
            grad_b_up.astype(jnp.bfloat16), "wide", scatter_dimension=0, tiled=True
        ).astype(jnp.float32),
        lax.psum_scatter(
            grad_w_down.astype(jnp.bfloat16), "wide", scatter_dimension=1, tiled=True
        ).astype(jnp.float32),
        lax.psum_scatter(
            grad_w_mod.astype(jnp.bfloat16), "wide", scatter_dimension=0, tiled=True
        ).astype(jnp.float32),
        lax.psum_scatter(
            grad_b_mod.astype(jnp.bfloat16), "wide", scatter_dimension=1, tiled=True
        ).astype(jnp.float32),
        lax.psum_scatter(
            grad_table.astype(jnp.bfloat16), "wide", scatter_dimension=1, tiled=True
        ).astype(jnp.float32),
    )
    return (
        result,
        grad_tokens,
        grad_noise,
        summed[7],
        summed[0],
        summed[1],
        summed[2],
        summed[3],
        summed[4],
        summed[5],
        summed[6],
    )


def solution(mesh):
    in_specs = (
        P("wide", None),
        P("wide", None),
        P("wide", None),
        P("wide", None),
        P("wide", None),
        P("wide", None),
        P(),
        P(None, None, "narrow"),
        P("narrow", None),
        P(None, "narrow"),
        P("narrow"),
        P("narrow", None),
        P(None, None, "narrow"),
        P(None, "narrow"),
    )
    out_specs = (
        P("wide", None),
        P("wide", None),
        P("wide", None),
        P(None, "wide"),
        P(None, "wide", "narrow"),
        P("narrow", "wide"),
        P("wide", "narrow"),
        P(("narrow", "wide")),
        P("narrow", "wide"),
        P("wide", None, "narrow"),
        P(None, ("narrow", "wide")),
    )
    return jax.shard_map(body, mesh=mesh, in_specs=in_specs, out_specs=out_specs, check_vma=False)
```

profile of v0, /device:TPU:0, one launch (start us, length us, event | category | flops | bytes accessed | tf_op | source)
XLA Modules:
  0.0 1386.5 jit_solution(8295451466740319210)
XLA Ops:
  7.3 2.9 convert_reduce_fusion
  10.2 3.4 fusion.29
  13.7 17.1 %copy.59 = bf16[2048,6,512]{0,2,1:T(8,128)(2,1)} copy(bf16[2048,6,512]{2,0,1:T(8,128)(2,1)} %param.30) | data formatting | bytes 25165824 | tf_op args[12]
  31.8 7.9 convolution_add_fusion
  39.8 15.2 %all_gather.3 = f32[16,6,2048]{2,1,0:T(8,128)S(1)} all-gather(f32[16,6,512]{2,1,0:T(8,128)S(1)} %reshape.223), channel_id=1, replica_groups=mesh['wide'=8,'narrow'=4] {'narrow'}, dimensions={2}, use_global_device_ids=true | all-gather | bytes 983040 | tf_op jit(solution)/shard_map/all_gather | solution.py:60
  56.5 3.6 fusion.89
  60.2 6.3 add_convert_fusion.3
  69.0 3.4 fusion.68
  72.4 3.3 multiply_convert_fusion.4
  83.1 19.1 %while.27 = (s32[]{:T(128)}, bf16[2,512,4,128]{3,2,1,0:T(4,128)(2,1)}, f32[2,4,512]{2,1,0:T(4,128)}, f32[2,512]{1,0:T(2,128)S(1)}, f32[1024]{0:T(1024)S(1)}, /*i...) while((s32[]{:T(128)}, ...), condition=%wide.region_5.6_spmd, body=%wide.region_2.5_spmd.sunk | while | flops 1093400576 | bytes 44247296 | solution.py:103
  83.7 2.6 select_reduce_fusion.2
  88.4 2.7 fusion.171
  93.1 2.6 select_reduce_fusion.2
  97.9 2.7 fusion.171
  102.2 7.3 fusion.75
  109.6 7.1 fusion.81
  116.7 5.9 fusion.84
  122.5 159.6 %all-reduce.7.cloned.1.call-done = f32[1024,2048]{1,0:T(8,128)} async-done(((f32[1024,2048]{1,0:T(8,128)}), f32[1024,2048]{1,0:T(8,128)}) %all-reduce.7.cloned.1.call-update) | async-done | bytes 8388624 | tf_op jit(solution)/shard_map/psum | solution.py:105
  282.1 9.8 fusion.115
  292.9 4.8 subtract_multiply_fusion
  301.2 6.9 add_convert_fusion.2
  308.1 31.0 %fusion.32 = (bf16[1024,2048]{1,0:T(8,128)(2,1)}, f32[1024,2048]{1,0:T(8,128)}) fusion(f32[2048]{0:T(1024)S(1)} %copy-done.53, bf16[1024,2048]{1,0:T(8,128)(2,1)S(1)} %add_convert_fusion.2, bf16[2048,2048]{1,0:T(8,128)(2,1)} %param.27), kind=kOutput, calls=%fused_computation.52 | convolution fusion | flops 8728346624 | bytes 25174016 | tf_op jit(solution)/shard_map/dot_general | solution.py:109
  339.1 20.5 %fusion.117 = (bf16[2048]{0:T(1024)(128)(2,1)}, bf16[1024,2048]{1,0:T(8,128)(2,1)}) fusion(f32[1024,2048]{1,0:T(8,128)} %get-tuple-element.305, f32[2048]{0:T(1024)S(1)} %copy-done.53, bf16[2048,2048]{1,0:T(8,128)(2,1)} %param.29, f32[1024,2048]{1,0:T(8,128)} %fusion.84, bf16[1024,2048]{1,0:T(8,128)(2,1)} %param.19), kind=kOutput, calls=%fused_computation.182 | convolution fusion | flops 8625584128 | bytes 33566720 | tf_op jit(solution)/shard_map/dot_general | solution.py:117
  359.6 14.7 %fusion.119 = f32[1024,2048]{1,0:T(8,128)} fusion(bf16[1024,2048]{1,0:T(8,128)(2,1)} %get-tuple-element.307, bf16[2048,2048]{1,0:T(8,128)(2,1)} %param.27), kind=kOutput, calls=%fused_computation.185 | convolution fusion | flops 8589934592 | bytes 20971520 | tf_op jit(solution)/shard_map/dot_general | solution.py:122
  374.4 13.8 convolution_convert_fusion.3
  388.2 159.1 %all-reduce.9.cloned.1.call-done = f32[1024,2048]{1,0:T(8,128)} async-done(((f32[1024,2048]{1,0:T(8,128)}), f32[1024,2048]{1,0:T(8,128)}) %all-reduce.9.cloned.1.call-update) | async-done | bytes 8388624 | tf_op jit(solution)/shard_map/psum | solution.py:122
  547.2 9.5 fusion.114
  556.7 18.6 %multiply_convert_fusion.1 = (bf16[1024,2048]{1,0:T(8,128)(2,1)}, f32[1024,2048]{1,0:T(8,128)}) fusion(f32[1024,2048]{1,0:T(8,128)} %get-tuple-element.303, f32[1024]{0:T(1024)S(1)} %get-tuple-element.310, f32[1024]{0:T(1024)S(1)} %get-tuple-element.311, f32[1024,2048]{1,0:T(8,128)} %all-reduce.9.cloned.1.call-done, f32[1024,2048]{1,0:T(8,128)} %fusion.81, ...), kind=kLoop, calls=%fused_computation.62 | loop fusion | flops 25165824 | bytes 50348032 | tf_op jit(solution)/shard_map/convert_element_type | solution.py:124
  575.4 5.6 convolution_convert_fusion.6
  583.2 33.3 %while.28 = (s32[]{:T(128)}, f32[1024,4,128]{0,2,1:T(8,128)}, f32[1024,4,128]{0,2,1:T(8,128)}, f32[2,512,4,128]{3,1,2,0:T(8,128)}, bf16[2,512,4,128]{3,1,2,0:T(8...) while((s32[]{:T(128)}, f32[1024,4,128]{0,2,1:T(8,128)}, ...), condition=%wide.region_15.16_spmd.clone, body=%wide.region_13.15_spmd.clone.sunk | while | flops 2712139776 | bytes 139528592 | solution.py:146
  587.8 2.5 bitcast_add_fusion.5
  590.3 3.3 multiply_reduce_fusion.5
  604.2 2.5 bitcast_add_fusion.5
  606.8 3.3 multiply_reduce_fusion.5
  624.0 10.9 bitcast_convert_fusion
  634.9 6.9 convert_element_type.188
  641.8 166.5 %all-reduce.13.cloned.1.call-done = (bf16[1024,2048]{1,0:T(8,128)(2,1)}, bf16[1024,2048]{1,0:T(8,128)(2,1)}) async-done(((bf16[1024,2048]{1,0:T(8,128)(2,1)}, bf16[1024,2048]{1,0:T(8,128)(2,1)}), (bf16[1024,2048]{1,0:T(8,128)(2,1)}, bf16[1024,2048]{1,0:T(8,128)(2,1)})) %all-reduce.13.cloned.1.call-update) | async-done | bytes 8388624 | tf_op jit(solution)/shard_map/psum | solution.py:111
  808.3 3.3 convert_element_type.202
  813.0 7.8 fusion.62
  823.5 3.9 fusion.55
  827.4 4.1 fusion.53
  833.1 3.5 fusion.51
  836.6 3.6 fusion.49
  840.2 7.2 fusion.118
  847.5 4.0 fusion.47
  851.6 5.9 convolution_convert_fusion.4
  857.5 14.3 %convolution_convert_fusion.1 = bf16[2048,2048]{1,0:T(8,128)(2,1)} fusion(bf16[1024,2048]{1,0:T(8,128)(2,1)} %copy-done.19, bf16[1024,2048]{1,0:T(8,128)(2,1)} %get-tuple-element.307), kind=kOutput, calls=%fused_computation.89 | convolution fusion | flops 8594128896 | bytes 16777216 | tf_op jit(solution)/shard_map/dot_general | solution.py:121
  871.9 15.3 %convolution_convert_fusion = bf16[2048,2048]{1,0:T(8,128)(2,1)} fusion(bf16[1024,2048]{1,0:T(8,128)(2,1)} %get-tuple-element.304, f32[1024,2048]{1,0:T(8,128)} %fusion.84, bf16[1024,2048]{1,0:T(8,128)(2,1)} %param.19), kind=kOutput, calls=%fused_computation.88 | convolution fusion | flops 8600420352 | bytes 25165824 | tf_op jit(solution)/shard_map/dot_general | solution.py:120
  888.2 5.7 all-reduce.11.cloned.1.call-done
  896.2 11.3 convert_bitcast_fusion
  907.6 6.5 convolution_convert_fusion.2
  916.0 16.1 %all-reduce = bf16[2048]{0:T(1024)(128)(2,1)S(1)} all-reduce(bf16[2048]{0:T(1024)(128)(2,1)S(1)} %copy-done.47), channel_id=6, replica_groups=mesh['wide'=8,'narrow'=4] {'wide'}, use_global_device_ids=true, to_apply=%region_25.26.clone | all-reduce | flops 2048 | bytes 8192
  934.5 88.3 %reduce-scatter.16.cloned.1.call-done = bf16[256,2048]{1,0:T(8,128)(2,1)} async-done(((bf16[2048,2048]{1,0:T(8,128)(2,1)}), bf16[256,2048]{1,0:T(8,128)(2,1)}) %reduce-scatter.16.cloned.1.call-update) | async-done | bytes 1048592 | tf_op jit(solution)/shard_map/reduce_scatter | solution.py:199
  1022.8 2.8 convert_element_type.215
  1025.6 87.5 %reduce-scatter.18.cloned.1.call-done = bf16[2048,256]{1,0:T(8,128)(2,1)} async-done(((bf16[2048,2048]{1,0:T(8,128)(2,1)}), bf16[2048,256]{1,0:T(8,128)(2,1)}) %reduce-scatter.18.cloned.1.call-update) | async-done | bytes 1048592 | tf_op jit(solution)/shard_map/reduce_scatter | solution.py:205
  1113.1 2.7 convert_element_type.218
  1115.8 11.6 add_convert_fusion.1
  1127.3 12.2 add_convert_fusion
  1139.5 4.3 reduce-scatter.24.cloned.1.call-done
  1145.3 30.6 %reduce-scatter.22.cloned.1.call-done = bf16[256,3]{1,0:T(8,128)(2,1)} async-done(((bf16[2048,3]{1,0:T(8,128)(2,1)}), bf16[256,3]{1,0:T(8,128)(2,1)}) %reduce-scatter.22.cloned.1.call-update) | async-done | bytes 1552
  1177.4 68.7 %reduce-scatter.12.cloned.1.call-done = bf16[3,256,512]{1,2,0:T(8,128)(2,1)} async-done(((bf16[3,2048,512]{1,2,0:T(8,128)(2,1)}), bf16[3,256,512]{1,2,0:T(8,128)(2,1)}) %reduce-scatter.12.cloned.1.call-update) | async-done | bytes 786448 | tf_op jit(solution)/shard_map/reduce_scatter | solution.py:193
  1246.1 2.6 copy.74
  1248.7 127.4 %reduce-scatter.20.cloned.1.call-done = bf16[256,6,512]{2,0,1:T(8,128)(2,1)} async-done(((bf16[2048,6,512]{2,0,1:T(8,128)(2,1)}), bf16[256,6,512]{2,0,1:T(8,128)(2,1)}) %reduce-scatter.20.cloned.1.call-update) | async-done | bytes 1572880 | tf_op jit(solution)/shard_map/reduce_scatter | solution.py:208
  1376.0 3.5 convert_element_type.220
  (256 shorter events, 71.5 us)
Async XLA Ops:
  7.2 95.0 %copy-start = (bf16[512,2048]{1,0:T(8,128)(2,1)S(1)}, bf16[512,2048]{1,0:T(8,128)(2,1)}, u32[]{:S(2)}) copy-start(bf16[512,2048]{1,0:T(8,128)(2,1)} %param.26) | copy-start | bytes 6291460
  7.2 6.5 copy-start.46
  7.2 274.9 %all-reduce.7.cloned.1.call-start = ((), (), s32[]{:S(2)}) async-start(), calls=%async_computation.7 | async-start | bytes 16777216 | tf_op jit(solution)/shard_map/psum | solution.py:105
  10.2 49.9 %copy-start.37 = (f32[1024]{0:T(1024)}, f32[1024]{0:T(1024)S(1)}, u32[]{:S(2)}) copy-start(f32[1024]{0:T(1024)S(1)} %broadcast_multiply_fusion.5) | copy-start | bytes 12292
  13.7 46.5 %copy-start.39 = (f32[1024]{0:T(1024)}, f32[1024]{0:T(1024)S(1)}, u32[]{:S(2)}) copy-start(f32[1024]{0:T(1024)S(1)} %add_rsqrt_fusion.1) | copy-start | bytes 12292
  13.7 17.1 %copy-start.33 = (f32[16,2048]{1,0:T(8,128)S(1)}, f32[16,2048]{1,0:T(8,128)}, u32[]{:S(2)}) copy-start(f32[16,2048]{1,0:T(8,128)} %param.20) | copy-start | bytes 393220
  13.7 17.1 %copy-start.45 = (f32[3,2048]{1,0:T(4,128)S(1)}, f32[3,2048]{1,0:T(4,128)}, u32[]{:S(2)}) copy-start(f32[3,2048]{1,0:T(4,128)} %param.24) | copy-start | bytes 73732
  13.7 17.1 %copy-start.48 = (s32[1,16]{1,0:T(1,128)S(1)}, s32[1,16]{1,0:T(1,128)}, u32[]{:S(2)}) copy-start(s32[1,16]{1,0:T(1,128)} %param.23) | copy-start | bytes 196
  30.8 25.4 %copy-start.41 = (s32[1,16]{1,0:T(1,128)S(1)}, s32[1,16]{1,0:T(1,128)}, u32[]{:S(2)}) copy-start(s32[1,16]{1,0:T(1,128)} %param.21) | copy-start | bytes 196
  30.8 25.4 %copy-start.54 = (s32[1,16]{1,0:T(1,128)S(1)}, s32[1,16]{1,0:T(1,128)}, u32[]{:S(2)}) copy-start(s32[1,16]{1,0:T(1,128)} %param.22) | copy-start | bytes 196
  39.8 20.4 %copy-start.7 = (bf16[1024,2048]{1,0:T(8,128)(2,1)S(1)}, bf16[1024,2048]{1,0:T(8,128)(2,1)}, u32[]{:S(2)}) copy-start(bf16[1024,2048]{1,0:T(8,128)(2,1)} %param.18) | copy-start | bytes 12582916
  56.3 243.9 %copy-start.43 = (s32[16]{0:T(128)}, s32[16]{0:T(128)S(1)}, u32[]{:S(2)}) copy-start(s32[16]{0:T(128)S(1)} %add_bitcast_fusion) | copy-start | bytes 196
  56.5 10.1 slice-start.7
  60.1 6.4 copy-start.3
  60.2 6.4 slice-start.8
  66.6 5.9 copy-start.18
  83.7 4.8 copy-start.15
  93.1 4.8 copy-start.15
  102.2 7.3 copy-start.9
  102.2 7.3 copy-start.29
  102.2 7.4 copy-start.31
  109.5 437.7 %all-reduce.9.cloned.1.call-start = ((), (), s32[]{:S(2)}) async-start(), calls=%async_computation.8 | async-start | bytes 16777216 | tf_op jit(solution)/shard_map/psum | solution.py:122
  291.9 8.2 copy-start.2
  291.9 8.2 slice-start
  292.9 8.3 slice-start.1
  301.2 6.9 copy-start.53
  308.1 31.0 %copy-start.19 = (bf16[1024,2048]{1,0:T(8,128)(2,1)}, bf16[1024,2048]{1,0:T(8,128)(2,1)S(1)}, u32[]{:S(2)}) copy-start(bf16[1024,2048]{1,0:T(8,128)(2,1)S(1)} %add_convert_fusion.2) | copy-start | bytes 12582916
  374.3 434.0 %all-reduce.13.cloned.1.call-start = ((), (), s32[]{:S(2)}) async-start(), calls=%async_computation.17 | async-start | bytes 16777216 | tf_op jit(solution)/shard_map/psum | solution.py:111
  575.3 7.9 copy-start.10
  575.3 7.9 copy-start.30
  575.3 7.9 copy-start.32
  575.3 7.9 copy-start.36
  583.6 4.2 copy-start.12
  600.1 4.1 copy-start.12
  616.5 4.0 copy-start.6
  621.2 13.6 copy-start.25
  623.9 10.9 copy-start.27
  634.8 259.0 %all-reduce.11.cloned.1.call-start = ((), (), s32[]{:S(2)}) async-start(), calls=%async_computation.9 | async-start | bytes 131072 | tf_op jit(solution)/shard_map/psum | solution.py:179
  641.8 169.9 %copy-start.38 = (f32[1024]{0:T(1024)S(1)}, f32[1024]{0:T(1024)}, u32[]{:S(2)}) copy-start(f32[1024]{0:T(1024)} %copy-done.37) | copy-start | bytes 12292
  641.8 169.9 %copy-start.40 = (f32[1024]{0:T(1024)S(1)}, f32[1024]{0:T(1024)}, u32[]{:S(2)}) copy-start(f32[1024]{0:T(1024)} %copy-done.39) | copy-start | bytes 12292
  808.3 3.4 copy-start.8
  808.3 4.7 copy-start.14
  813.0 7.8 copy-start.17
  821.9 9.5 slice-start.2
  823.5 7.9 slice-start.3
  831.5 8.8 copy-start.42
  831.5 8.8 copy-start.44
  833.1 14.4 %slice-start.4 = ((s8[12582912]{0:T(1024)(128)(4,1)}), s8[4194304]{0:T(1024)(128)(4,1)S(1)}, s32[]{:S(2)}) async-start(s8[12582912]{0:T(1024)(128)(4,1)} %bitcast.222), calls=%async_computation.22 | async-start | bytes 8388608
  836.6 10.9 slice-start.5
  840.2 7.3 slice-start.6
  847.4 4.1 copy-start.52
  851.5 81.3 %reduce-scatter.14.cloned.1.call-start = ((), (), s32[]{:S(2)}) async-start(), calls=%async_computation.11 | async-start | bytes 2359296 | tf_op jit(solution)/shard_map/reduce_scatter | solution.py:196
  857.5 165.3 %reduce-scatter.16.cloned.1.call-start = ((), (), s32[]{:S(2)}) async-start(), calls=%async_computation.12 | async-start | bytes 9437184 | tf_op jit(solution)/shard_map/reduce_scatter | solution.py:199
  871.8 241.3 %reduce-scatter.18.cloned.1.call-start = ((), (), s32[]{:S(2)}) async-start(), calls=%async_computation.13 | async-start | bytes 9437184 | tf_op jit(solution)/shard_map/reduce_scatter | solution.py:205
  887.2 6.6 copy-start.21
  887.2 7.5 copy-start.49
  887.2 9.0 copy-start.24
  887.2 9.0 copy-start.26
  887.2 256.6 %reduce-scatter.24.cloned.1.call-start = ((), (), s32[]{:S(2)}) async-start(), calls=%async_computation.16 | async-start | bytes 147456
  888.1 287.8 %reduce-scatter.22.cloned.1.call-start = ((), (), s32[]{:S(2)}) async-start(), calls=%async_computation.15 | async-start | bytes 589824
  894.7 12.8 copy-start.28
  896.1 350.0 %reduce-scatter.12.cloned.1.call-start = ((), (), s32[]{:S(2)}) async-start(), calls=%async_computation.10 | async-start | bytes 7077888 | tf_op jit(solution)/shard_map/reduce_scatter | solution.py:193
  907.6 468.5 %reduce-scatter.20.cloned.1.call-start = ((), (), s32[]{:S(2)}) async-start(), calls=%async_computation.14 | async-start | bytes 14155776 | tf_op jit(solution)/shard_map/reduce_scatter | solution.py:208
  1127.3 252.2 %copy-start.1 = (bf16[512,2048]{1,0:T(8,128)(2,1)S(1)}, bf16[512,2048]{1,0:T(8,128)(2,1)}, u32[]{:S(2)}) copy-start(bf16[512,2048]{1,0:T(8,128)(2,1)} %param.26) | copy-start | bytes 6291460
  (25 other events, 46.1 us)
Sparse Core Ops, SparseCore 0:
  109.6 172.4 all-reduce.6
  374.4 172.7 all-reduce.8
  635.0 173.3 all-reduce.12
  851.6 42.1 all-reduce.10
  896.5 35.7 reduce-scatter.13
  934.5 88.2 reduce-scatter.15
  1025.1 87.9 reduce-scatter.17
  1115.3 28.5 reduce-scatter.23
  1146.8 29.0 reduce-scatter.21
  1178.0 68.0 reduce-scatter.11
  1248.4 127.5 reduce-scatter.19
where the time goes:
time: 1390 us
  waiting for transfers between devices  898 us (65%)
  matrix products  257 us (18%)
  other arithmetic  126 us (9%)
  local copies, waits for them, and re-layouts  56.8 us (4%)
  blocking collectives  31.3 us (2%)
  between operations  15.7 us (1%)
    psum x1, waiting for transfers between devices, body(): lax.psum(jnp.dot(hidden, w_down, preferred_element_type=f32).astype(jnp.b...  167 us
    psum x1, waiting for transfers between devices, body(): lax.psum(jnp.dot(heads_out, w_out, preferred_element_type=f32), 'narrow')  160 us
    psum x1, waiting for transfers between devices, body(): lax.psum(jnp.dot(d_pre, w_up.T, preferred_element_type=f32), 'narrow')  159 us
    reduce_scatter x1, waiting for transfers between devices, body(): lax.psum_scatter(grad_w_mod.astype(jnp.bfloat16), 'wide', scatter_dimensi...  127 us
    reduce_scatter x1, waiting for transfers between devices, body(): lax.psum_scatter(grad_w_up.astype(jnp.bfloat16), 'wide', scatter_dimensio...  88.3 us
    reduce_scatter x1, waiting for transfers between devices, body(): lax.psum_scatter(grad_w_down.astype(jnp.bfloat16), 'wide', scatter_dimens...  87.5 us
    reduce_scatter x1, waiting for transfers between devices, body(): lax.psum_scatter(grad_w_qkv.astype(jnp.bfloat16), 'wide', scatter_dimensi...  68.7 us
    dot_general x6, matrix products, per_token(): return jnp.dot(member, mod_full[:, column], precision=highest)  39.6 us
  transfers between devices with their start and end apart: 11, of which 10 were waited for; matrix products, arithmetic and copies ran while one was open for 9% of the time, Pallas kernels for 0%

commit v1 on v0

--- a/solution.py
+++ b/solution.py
@@ -108,8 +108,12 @@
     mixed_b = (normed_b * (1.0 + scale_b) + shift_b).astype(half)
     hidden_pre = jnp.dot(mixed_b, w_up, preferred_element_type=f32) + b_up
     hidden = jax.nn.gelu(hidden_pre, approximate=False).astype(half)
-    mlp_out = lax.psum(
-        jnp.dot(hidden, w_down, preferred_element_type=f32).astype(jnp.bfloat16), "narrow"
+
+    def clear_frames_up(arr_in):
+        return jax.lax.all_gather(arr_in, "narrow").sum(axis=0)
+
+    mlp_out = clear_frames_up(
+        jnp.dot(hidden, w_down, preferred_element_type=f32).astype(jnp.bfloat16)
     ).astype(jnp.float32)
     result = (middle + gate_b * mlp_out).astype(half)
     grad_out = cotangent.astype(f32)

time: 1390 us -> 1520 us (1.094)
  waiting for transfers between devices: 898 us -> 1010 us
    all_gather x0 -> x1, waiting for transfers between devices: none -> 158 us  [clear_frames_up(): return jax.lax.all_gather(arr_in, 'narrow').sum(axis=0)]
    psum x1, waiting for transfers between devices: 167 us -> 91.4 us  [body(): lax.psum(jnp.einsum('tiv,idv->td', d_proj, w_qkv, preferred_element_type=...]
    psum x1, waiting for transfers between devices: 5.66 us -> 34.7 us  [body(): lax.psum(jnp.dot(flat_modes, w_mod.reshape(width, 6 * local_width).T, pre...]
    unnamed x13 -> x14, waiting for transfers between devices: 35.1 us -> 16.4 us
    unnamed x113 -> x119, local copies, waits for them, and re-layouts: 33.3 us -> 35.4 us
  transfers between devices with their start and end apart: 11 -> 12, of which waited for: 10 -> 10; matrix products, arithmetic and copies ran while one was open for 9% -> 7% of each run, Pallas kernels for 0% -> 0%
where the time goes in v1:
time: 1520 us; the launch traced here: 1510 us
  waiting for transfers between devices  1010 us (66%)
  matrix products  257 us (17%)
  other arithmetic  133 us (9%)
  local copies, waits for them, and re-layouts  59 us (4%)
  blocking collectives  31.3 us (2%)
  between operations  15.8 us (1%)
    psum x1, waiting for transfers between devices, body(): lax.psum(jnp.dot(d_pre, w_up.T, preferred_element_type=f32), 'narrow')  172 us
    psum x1, waiting for transfers between devices, body(): lax.psum(jnp.dot(heads_out, w_out, preferred_element_type=f32), 'narrow')  166 us
    all_gather x1, waiting for transfers between devices, clear_frames_up(): return jax.lax.all_gather(arr_in, 'narrow').sum(axis=0)  158 us
    reduce_scatter x1, waiting for transfers between devices, body(): lax.psum_scatter(grad_w_mod.astype(jnp.bfloat16), 'wide', scatter_dimensi...  127 us
    psum x1, waiting for transfers between devices, body(): lax.psum(jnp.einsum('tiv,idv->td', d_proj, w_qkv, preferred_element_type=...  91.4 us
    reduce_scatter x1, waiting for transfers between devices, body(): lax.psum_scatter(grad_w_up.astype(jnp.bfloat16), 'wide', scatter_dimensio...  88.6 us
    reduce_scatter x1, waiting for transfers between devices, body(): lax.psum_scatter(grad_w_down.astype(jnp.bfloat16), 'wide', scatter_dimens...  87.4 us
    reduce_scatter x1, waiting for transfers between devices, body(): lax.psum_scatter(grad_w_qkv.astype(jnp.bfloat16), 'wide', scatter_dimensi...  67.8 us
  transfers between devices with their start and end apart: 12, of which 10 were waited for; matrix products, arithmetic and copies ran while one was open for 7% of the time, Pallas kernels for 0%

profile of v1, /device:TPU:0, one launch (start us, length us, event | category | flops | bytes accessed | tf_op | source)
XLA Modules:
  0.0 1507.8 jit_solution(1222937744132881150)
XLA Ops:
  7.3 2.9 convert_reduce_fusion
  10.2 3.4 fusion.29
  13.7 17.1 %copy.59 = bf16[2048,6,512]{0,2,1:T(8,128)(2,1)} copy(bf16[2048,6,512]{2,0,1:T(8,128)(2,1)} %param.30) | data formatting | bytes 25165824 | tf_op args[12]
  31.7 7.9 convolution_add_fusion
  39.8 15.2 %all_gather.9 = f32[16,6,2048]{2,1,0:T(8,128)S(1)} all-gather(f32[16,6,512]{2,1,0:T(8,128)S(1)} %reshape.223), channel_id=1, replica_groups=mesh['wide'=8,'narrow'=4] {'narrow'}, dimensions={2}, use_global_device_ids=true | all-gather | bytes 983040 | tf_op jit(solution)/shard_map/all_gather | solution.py:60
  56.5 3.6 fusion.89
  60.2 6.4 add_convert_fusion.3
  69.0 3.4 fusion.68
  72.5 3.3 multiply_convert_fusion.4
  83.2 19.1 %while.27 = (s32[]{:T(128)}, bf16[2,512,4,128]{3,2,1,0:T(4,128)(2,1)}, f32[2,4,512]{2,1,0:T(4,128)}, f32[2,512]{1,0:T(2,128)S(1)}, f32[1024]{0:T(1024)S(1)}, /*i...) while((s32[]{:T(128)}, ...), condition=%wide.region_5.6_spmd, body=%wide.region_2.5_spmd.sunk | while | flops 1093400576 | bytes 44247296 | solution.py:103
  83.7 2.6 select_reduce_fusion.2
  88.5 2.7 fusion.171
  93.2 2.6 select_reduce_fusion.2
  98.0 2.7 fusion.171
  102.3 7.2 fusion.75
  109.6 6.1 fusion.81
  115.7 166.4 %all-reduce.6.cloned.1.call-done = f32[1024,2048]{1,0:T(8,128)} async-done(((f32[1024,2048]{1,0:T(8,128)}), f32[1024,2048]{1,0:T(8,128)}) %all-reduce.6.cloned.1.call-update) | async-done | bytes 8388624 | tf_op jit(solution)/shard_map/psum | solution.py:105
  282.1 9.8 fusion.115
  292.8 4.8 subtract_multiply_fusion
  301.1 7.0 add_convert_fusion.2
  308.2 31.2 %fusion.32 = (bf16[1024,2048]{1,0:T(8,128)(2,1)S(1)}, f32[1024,2048]{1,0:T(8,128)}) fusion(f32[2048]{0:T(1024)S(1)} %copy-done.53, bf16[1024,2048]{1,0:T(8,128)(2,1)S(1)} %add_convert_fusion.2, bf16[2048,2048]{1,0:T(8,128)(2,1)} %param.27), kind=kOutput, calls=%fused_computation.52 | convolution fusion | flops 8728346624 | bytes 25174016 | tf_op jit(solution)/shard_map/dot_general | solution.py:109
  341.4 10.3 convolution_convert_fusion.3
  351.8 158.2 %all-gather.3.cloned.1.call-done = bf16[4096,2048]{1,0:T(8,128)(2,1)} async-done(((bf16[1024,2048]{1,0:T(8,128)(2,1)}), bf16[4096,2048]{1,0:T(8,128)(2,1)}) %all-gather.3.cloned.1.call-update) | async-done | bytes 16777232 | tf_op jit(solution)/shard_map/all_gather | solution.py:113
  510.0 12.6 reduce_sum.130
  522.6 9.9 add_convert_fusion.1
  532.6 20.4 %fusion.117 = (bf16[2048]{0:T(1024)(128)(2,1)}, bf16[1024,2048]{1,0:T(8,128)(2,1)}) fusion(f32[1024,2048]{1,0:T(8,128)} %get-tuple-element.303, f32[2048]{0:T(1024)S(1)} %copy-done.53, bf16[2048,2048]{1,0:T(8,128)(2,1)} %param.29, f32[1024,2048]{1,0:T(8,128)} %get-tuple-element.305, bf16[1024,2048]{1,0:T(8,128)(2,1)} %param.19), kind=kOutput, calls=%fused_computation.182 | convolution fusion | flops 8625584128 | bytes 33566720 | tf_op jit(solution)/shard_map/dot_general | solution.py:121
  553.0 14.5 fusion.119
  567.6 172.2 %all-reduce.8.cloned.1.call-done = f32[1024,2048]{1,0:T(8,128)} async-done(((f32[1024,2048]{1,0:T(8,128)}), f32[1024,2048]{1,0:T(8,128)}) %all-reduce.8.cloned.1.call-update) | async-done | bytes 8388624 | tf_op jit(solution)/shard_map/psum | solution.py:126
  739.8 9.6 fusion.114
  749.5 18.6 %multiply_convert_fusion.1 = (bf16[1024,2048]{1,0:T(8,128)(2,1)}, f32[1024,2048]{1,0:T(8,128)}) fusion(f32[1024,2048]{1,0:T(8,128)} %get-tuple-element.301, f32[1024]{0:T(1024)S(1)} %get-tuple-element.310, f32[1024]{0:T(1024)S(1)} %get-tuple-element.311, f32[1024,2048]{1,0:T(8,128)} %all-reduce.8.cloned.1.call-done, f32[1024,2048]{1,0:T(8,128)} %fusion.81, ...), kind=kLoop, calls=%fused_computation.62 | loop fusion | flops 25165824 | bytes 50348032 | tf_op jit(solution)/shard_map/convert_element_type | solution.py:128
  768.1 5.6 convolution_convert_fusion.6
  775.9 32.9 %while.28 = (s32[]{:T(128)}, f32[1024,4,128]{0,2,1:T(8,128)}, f32[1024,4,128]{0,2,1:T(8,128)}, f32[2,512,4,128]{3,1,2,0:T(8,128)}, bf16[2,512,4,128]{3,1,2,0:T(8...) while((s32[]{:T(128)}, f32[1024,4,128]{0,2,1:T(8,128)}, ...), condition=%wide.region_15.16_spmd.clone, body=%wide.region_13.15_spmd.clone.sunk | while | flops 2712139776 | bytes 139528592 | solution.py:150
  780.1 2.5 bitcast_add_fusion.5
  782.7 3.3 multiply_reduce_fusion.5
  799.1 3.3 multiply_reduce_fusion.5
  816.3 10.9 bitcast_convert_fusion
  827.3 6.7 convert_element_type.190
  834.0 6.5 convert_element_type.188
  840.5 91.4 %all-reduce.10.cloned.1.call-done = bf16[1024,2048]{1,0:T(8,128)(2,1)} async-done(((bf16[1024,2048]{1,0:T(8,128)(2,1)}), bf16[1024,2048]{1,0:T(8,128)(2,1)}) %all-reduce.10.cloned.1.call-update) | async-done | bytes 4194320 | tf_op jit(solution)/shard_map/psum | solution.py:158
  931.9 3.3 convert_element_type.204
  936.9 8.2 fusion.62
  945.1 3.4 fusion.55
  948.5 4.1 fusion.53
  954.2 3.5 fusion.51
  957.7 4.3 fusion.49
  962.0 7.2 fusion.118
  969.3 4.0 fusion.47
  973.4 5.9 convolution_convert_fusion.4
  980.2 34.7 %all-reduce.12.cloned.1.call-done = bf16[16,2048]{1,0:T(8,128)(2,1)} async-done(((bf16[16,2048]{1,0:T(8,128)(2,1)}), bf16[16,2048]{1,0:T(8,128)(2,1)}) %all-reduce.12.cloned.1.call-update) | async-done | bytes 65552 | tf_op jit(solution)/shard_map/psum | solution.py:183
  1017.3 14.2 convolution_convert_fusion.1
  1031.6 15.4 %convolution_convert_fusion = bf16[2048,2048]{1,0:T(8,128)(2,1)} fusion(bf16[1024,2048]{1,0:T(8,128)(2,1)} %copy-done.56, f32[1024,2048]{1,0:T(8,128)} %get-tuple-element.305, bf16[1024,2048]{1,0:T(8,128)(2,1)} %param.19), kind=kOutput, calls=%fused_computation.88 | convolution fusion | flops 8600420352 | bytes 25165824 | tf_op jit(solution)/shard_map/dot_general | solution.py:124
  1048.6 11.2 convert_bitcast_fusion
  1059.9 6.5 convolution_convert_fusion.2
  1068.3 16.0 %all-reduce = bf16[2048]{0:T(1024)(128)(2,1)S(1)} all-reduce(bf16[2048]{0:T(1024)(128)(2,1)S(1)} %copy-done.47), channel_id=7, replica_groups=mesh['wide'=8,'narrow'=4] {'wide'}, use_global_device_ids=true, to_apply=%region_25.26.clone | all-reduce | flops 2048 | bytes 8192
  1086.8 12.2 add_convert_fusion
  1100.4 16.2 %reduce-scatter.22.cloned.1.call-done = bf16[256,3]{1,0:T(8,128)(2,1)} async-done(((bf16[2048,3]{1,0:T(8,128)(2,1)}), bf16[256,3]{1,0:T(8,128)(2,1)}) %reduce-scatter.22.cloned.1.call-update) | async-done | bytes 1552
  1118.2 88.6 %reduce-scatter.16.cloned.1.call-done = bf16[256,2048]{1,0:T(8,128)(2,1)} async-done(((bf16[2048,2048]{1,0:T(8,128)(2,1)}), bf16[256,2048]{1,0:T(8,128)(2,1)}) %reduce-scatter.16.cloned.1.call-update) | async-done | bytes 1048592 | tf_op jit(solution)/shard_map/reduce_scatter | solution.py:203
  1206.8 2.8 convert_element_type.217
  1209.6 87.4 %reduce-scatter.18.cloned.1.call-done = bf16[2048,256]{1,0:T(8,128)(2,1)} async-done(((bf16[2048,2048]{1,0:T(8,128)(2,1)}), bf16[2048,256]{1,0:T(8,128)(2,1)}) %reduce-scatter.18.cloned.1.call-update) | async-done | bytes 1048592 | tf_op jit(solution)/shard_map/reduce_scatter | solution.py:209
  1296.9 2.7 convert_element_type.220
  1299.6 67.8 %reduce-scatter.12.cloned.1.call-done = bf16[3,256,512]{1,2,0:T(8,128)(2,1)} async-done(((bf16[3,2048,512]{1,2,0:T(8,128)(2,1)}), bf16[3,256,512]{1,2,0:T(8,128)(2,1)}) %reduce-scatter.12.cloned.1.call-update) | async-done | bytes 786448 | tf_op jit(solution)/shard_map/reduce_scatter | solution.py:197
  1367.4 2.6 copy.74
  1370.0 127.2 %reduce-scatter.20.cloned.1.call-done = bf16[256,6,512]{2,0,1:T(8,128)(2,1)} async-done(((bf16[2048,6,512]{2,0,1:T(8,128)(2,1)}), bf16[256,6,512]{2,0,1:T(8,128)(2,1)}) %reduce-scatter.20.cloned.1.call-update) | async-done | bytes 1572880 | tf_op jit(solution)/shard_map/reduce_scatter | solution.py:212
  1497.2 3.5 convert_element_type.222
  (266 shorter events, 75.3 us)
Async XLA Ops:
  7.2 95.1 %copy-start = (bf16[512,2048]{1,0:T(8,128)(2,1)S(1)}, bf16[512,2048]{1,0:T(8,128)(2,1)}, u32[]{:S(2)}) copy-start(bf16[512,2048]{1,0:T(8,128)(2,1)} %param.26) | copy-start | bytes 6291460
  7.2 6.5 copy-start.46
  7.2 274.9 %all-reduce.6.cloned.1.call-start = ((), (), s32[]{:S(2)}) async-start(), calls=%async_computation.7 | async-start | bytes 16777216 | tf_op jit(solution)/shard_map/psum | solution.py:105
  10.2 49.9 %copy-start.37 = (f32[1024]{0:T(1024)}, f32[1024]{0:T(1024)S(1)}, u32[]{:S(2)}) copy-start(f32[1024]{0:T(1024)S(1)} %broadcast_multiply_fusion.5) | copy-start | bytes 12292
  13.7 46.5 %copy-start.39 = (f32[1024]{0:T(1024)}, f32[1024]{0:T(1024)S(1)}, u32[]{:S(2)}) copy-start(f32[1024]{0:T(1024)S(1)} %add_rsqrt_fusion.1) | copy-start | bytes 12292
  13.7 17.1 %copy-start.33 = (f32[16,2048]{1,0:T(8,128)S(1)}, f32[16,2048]{1,0:T(8,128)}, u32[]{:S(2)}) copy-start(f32[16,2048]{1,0:T(8,128)} %param.20) | copy-start | bytes 393220
  13.7 17.1 %copy-start.45 = (f32[3,2048]{1,0:T(4,128)S(1)}, f32[3,2048]{1,0:T(4,128)}, u32[]{:S(2)}) copy-start(f32[3,2048]{1,0:T(4,128)} %param.24) | copy-start | bytes 73732
  13.7 17.1 %copy-start.48 = (s32[1,16]{1,0:T(1,128)S(1)}, s32[1,16]{1,0:T(1,128)}, u32[]{:S(2)}) copy-start(s32[1,16]{1,0:T(1,128)} %param.23) | copy-start | bytes 196
  30.8 25.4 %copy-start.41 = (s32[1,16]{1,0:T(1,128)S(1)}, s32[1,16]{1,0:T(1,128)}, u32[]{:S(2)}) copy-start(s32[1,16]{1,0:T(1,128)} %param.21) | copy-start | bytes 196
  30.8 25.4 %copy-start.54 = (s32[1,16]{1,0:T(1,128)S(1)}, s32[1,16]{1,0:T(1,128)}, u32[]{:S(2)}) copy-start(s32[1,16]{1,0:T(1,128)} %param.22) | copy-start | bytes 196
  39.8 20.4 %copy-start.7 = (bf16[1024,2048]{1,0:T(8,128)(2,1)S(1)}, bf16[1024,2048]{1,0:T(8,128)(2,1)}, u32[]{:S(2)}) copy-start(bf16[1024,2048]{1,0:T(8,128)(2,1)} %param.18) | copy-start | bytes 12582916
  56.2 466.4 %copy-start.43 = (s32[16]{0:T(128)}, s32[16]{0:T(128)S(1)}, u32[]{:S(2)}) copy-start(s32[16]{0:T(128)S(1)} %add_bitcast_fusion) | copy-start | bytes 196
  56.4 10.1 slice-start.9
  60.1 6.4 copy-start.3
  60.1 6.4 slice-start.10
  66.6 5.9 copy-start.17
  83.7 4.8 copy-start.15
  93.2 4.8 copy-start.15
  102.3 7.3 copy-start.9
  102.3 7.3 copy-start.29
  102.3 7.3 copy-start.31
  109.6 400.4 %all-gather.3.cloned.1.call-start = ((), (), s32[]{:S(2)}) async-start(), calls=%async_computation.16 | async-start | bytes 20971520 | tf_op jit(solution)/shard_map/all_gather | solution.py:113
  291.8 8.2 copy-start.2
  291.8 8.2 slice-start
  292.8 8.3 slice-start.1
  301.1 7.1 copy-start.53
  301.1 40.3 %slice-start.7 = ((s8[8388608]{0:T(1024)(128)(4,1)}), s8[4194304]{0:T(1024)(128)(4,1)S(1)}, s32[]{:S(2)}) async-start(s8[8388608]{0:T(1024)(128)(4,1)} %bitcast.251), calls=%async_computation.26 | async-start | bytes 8388608
  308.2 31.2 %copy-start.18 = (bf16[1024,2048]{1,0:T(8,128)(2,1)}, bf16[1024,2048]{1,0:T(8,128)(2,1)S(1)}, u32[]{:S(2)}) copy-start(bf16[1024,2048]{1,0:T(8,128)(2,1)S(1)} %add_convert_fusion.2) | copy-start | bytes 12582916
  308.2 33.2 %slice-start.8 = ((s8[8388608]{0:T(1024)(128)(4,1)}), s8[4194304]{0:T(1024)(128)(4,1)S(1)}, s32[]{:S(2)}) async-start(s8[8388608]{0:T(1024)(128)(4,1)} %bitcast.251), calls=%async_computation.27 | async-start | bytes 8388608
  351.7 388.1 %all-reduce.8.cloned.1.call-start = ((), (), s32[]{:S(2)}) async-start(), calls=%async_computation.8 | async-start | bytes 16777216 | tf_op jit(solution)/shard_map/psum | solution.py:126
  510.0 12.6 copy-start.27
  567.5 364.4 %all-reduce.10.cloned.1.call-start = ((), (), s32[]{:S(2)}) async-start(), calls=%async_computation.9 | async-start | bytes 8388608 | tf_op jit(solution)/shard_map/psum | solution.py:158
  768.1 7.8 copy-start.10
  768.1 7.8 copy-start.30
  768.1 7.8 copy-start.32
  768.1 7.8 copy-start.36
  775.9 4.2 copy-start.12
  792.4 4.1 copy-start.12
  813.6 13.7 copy-start.24
  816.2 11.0 copy-start.26
  827.2 187.7 %all-reduce.12.cloned.1.call-start = ((), (), s32[]{:S(2)}) async-start(), calls=%async_computation.10 | async-start | bytes 131072 | tf_op jit(solution)/shard_map/psum | solution.py:183
  840.5 96.4 %copy-start.38 = (f32[1024]{0:T(1024)S(1)}, f32[1024]{0:T(1024)}, u32[]{:S(2)}) copy-start(f32[1024]{0:T(1024)} %copy-done.37) | copy-start | bytes 12292
  840.5 96.4 %copy-start.40 = (f32[1024]{0:T(1024)S(1)}, f32[1024]{0:T(1024)}, u32[]{:S(2)}) copy-start(f32[1024]{0:T(1024)} %copy-done.39) | copy-start | bytes 12292
  931.9 4.9 copy-start.8
  931.9 5.0 copy-start.14
  935.3 17.3 %slice-start.2 = ((s8[8388608]{0:T(1024)(128)(4,1)}), s8[4194304]{0:T(1024)(128)(4,1)S(1)}, s32[]{:S(2)}) async-start(s8[8388608]{0:T(1024)(128)(4,1)} %bitcast.223), calls=%async_computation.21 | async-start | bytes 8388608
  936.9 15.7 %slice-start.3 = ((s8[8388608]{0:T(1024)(128)(4,1)}), s8[4194304]{0:T(1024)(128)(4,1)S(1)}, s32[]{:S(2)}) async-start(s8[8388608]{0:T(1024)(128)(4,1)} %bitcast.223), calls=%async_computation.22 | async-start | bytes 8388608
  952.6 9.5 copy-start.42
  952.6 9.5 copy-start.44
  954.2 15.1 slice-start.4
  957.7 11.5 slice-start.5
  962.0 7.3 slice-start.6
  969.3 4.1 copy-start.52
  973.3 41.7 %copy-start.20 = (f32[16,2048]{1,0:T(8,128)S(1)}, f32[16,2048]{1,0:T(8,128)}, u32[]{:S(2)}) copy-start(f32[16,2048]{1,0:T(8,128)} %copy-done.19) | copy-start | bytes 393220
  973.3 42.6 %copy-start.49 = (s32[1,16]{1,0:T(1,128)S(1)}, s32[1,16]{1,0:T(1,128)}, u32[]{:S(2)}) copy-start(s32[1,16]{1,0:T(1,128)} %param.23) | copy-start | bytes 196
  973.3 111.7 %reduce-scatter.14.cloned.1.call-start = ((), (), s32[]{:S(2)}) async-start(), calls=%async_computation.12 | async-start | bytes 2359296 | tf_op jit(solution)/shard_map/reduce_scatter | solution.py:200
  979.3 119.7 %reduce-scatter.24.cloned.1.call-start = ((), (), s32[]{:S(2)}) async-start(), calls=%async_computation.18 | async-start | bytes 147456
  980.2 136.5 %reduce-scatter.22.cloned.1.call-start = ((), (), s32[]{:S(2)}) async-start(), calls=%async_computation.17 | async-start | bytes 589824
  1015.9 15.7 %copy-start.28 = (f32[16,2048]{1,0:T(8,128)}, f32[16,2048]{1,0:T(8,128)S(1)}, u32[]{:S(2)}) copy-start(f32[16,2048]{1,0:T(8,128)S(1)} %add_multiply_fusion.2) | copy-start | bytes 393220
  1017.3 189.5 %reduce-scatter.16.cloned.1.call-start = ((), (), s32[]{:S(2)}) async-start(), calls=%async_computation.13 | async-start | bytes 9437184 | tf_op jit(solution)/shard_map/reduce_scatter | solution.py:203
  1031.6 265.4 %reduce-scatter.18.cloned.1.call-start = ((), (), s32[]{:S(2)}) async-start(), calls=%async_computation.14 | async-start | bytes 9437184 | tf_op jit(solution)/shard_map/reduce_scatter | solution.py:209
  1047.1 320.4 %reduce-scatter.12.cloned.1.call-start = ((), (), s32[]{:S(2)}) async-start(), calls=%async_computation.11 | async-start | bytes 7077888 | tf_op jit(solution)/shard_map/reduce_scatter | solution.py:197
  1059.9 437.3 %reduce-scatter.20.cloned.1.call-start = ((), (), s32[]{:S(2)}) async-start(), calls=%async_computation.15 | async-start | bytes 14155776 | tf_op jit(solution)/shard_map/reduce_scatter | solution.py:212
  1086.8 413.9 %copy-start.1 = (bf16[512,2048]{1,0:T(8,128)(2,1)S(1)}, bf16[512,2048]{1,0:T(8,128)(2,1)}, u32[]{:S(2)}) copy-start(bf16[512,2048]{1,0:T(8,128)(2,1)} %param.26) | copy-start | bytes 6291460
  (29 other events, 54.9 us)
Sparse Core Ops, SparseCore 0:
  109.7 172.3 all-reduce.5
  351.9 158.0 all-gather.2
  567.6 172.1 all-reduce.7
  827.4 104.5 all-reduce.9
  973.4 41.4 all-reduce.11
  1017.7 35.7 reduce-scatter.13
  1055.7 28.8 reduce-scatter.23
  1087.5 29.0 reduce-scatter.21
  1118.9 87.8 reduce-scatter.15
  1208.9 87.9 reduce-scatter.17
  1299.3 68.1 reduce-scatter.11
  1369.6 127.5 reduce-scatter.19
